TPU v7x, 32 devices: a whole 2x2x4 slice. The times are simulated.
32 devices in a mesh: rep: 8 (over z, x), batch: 4 (over y, core).
Axes of the slice: x: 2, y: 2, z: 4, core: 2. Of those that a mesh axis runs over, the one named last changes fastest.
Arguments:
- embed: bfloat16 [4096, 1024], P(('rep', 'batch')), may hold values from -9 to 9
- actions: int32 [4096, 5], P(('rep', 'batch')), may hold values from 0 to 17
- rewards: float32 [4096, 5], P(('rep', 'batch')), may hold values from -1 to 1
- ends: int32 [4096, 5], P(('rep', 'batch')), may hold values 0 or 1
- behaviour: float32 [4096, 5, 18], P(('rep', 'batch')), may hold values from -5 to 5
- w_hidden: bfloat16 [1024, 1024], replicated, may hold values from -0.1875 to 0.1875
- w_action: bfloat16 [18, 1024], replicated, may hold values from -3 to 3
- w_heads: bfloat16 [1024, 36], replicated, may hold values from -0.1875 to 0.1875
Outputs:
- grad_hidden: float32 [1024, 1024], replicated
- grad_action: float32 [18, 1024], replicated
- grad_heads: float32 [1024, 36], replicated
- targets: float32 [4096, 5], P(('rep', 'batch'))
All inputs are finite; a program needn't handle non-finite values. No bound on the sum of `ends` on one device may be relied on, other than what follows from the above.
Results may differ from a plain program's by a relative error of at most 0.0057.
Values sent between devices are 32-bit elements; how exact they have to be, the bound alone decides.
A program may use at most 64 MiB of HBM per device.

v0:
```python
import jax
import jax.numpy as jnp
from jax import lax
from jax.sharding import PartitionSpec as P

DISCOUNT = 0.997
TRACE_LAMBDA = 0.95
EPSILON = 1e-06


def unroll(emb_block, act_block, w_hidden, w_action, w_heads):
    act_count = w_action.shape[0]
    unroll_len = act_block.shape[1]
    onehot = (
        act_block[:, :, None] == jnp.arange(act_count, dtype=jnp.int32)[None, None, :]
    ).astype(jnp.bfloat16)
    hidden_state = emb_block.astype(jnp.float32)
    rounded = []
    squashed = []
    head_out = []
    for step in range(unroll_len):
        state_bf16 = hidden_state.astype(jnp.bfloat16)
        rounded.append(state_bf16)
        head_out.append(jnp.dot(state_bf16, w_heads, preferred_element_type=jnp.float32))
        preact = jnp.dot(state_bf16, w_hidden, preferred_element_type=jnp.float32)
        preact = preact + jnp.dot(onehot[:, step], w_action, preferred_element_type=jnp.float32)
        squash = jnp.tanh(preact)
        squashed.append(squash)
        hidden_state = hidden_state + squash
    state_bf16 = hidden_state.astype(jnp.bfloat16)
    head_out.append(jnp.dot(state_bf16, w_heads, preferred_element_type=jnp.float32))
    return (jnp.stack(head_out), rounded, squashed, onehot)


def estimates(head_out, actions, rewards, ends, behaviour):
    act_count = behaviour.shape[-1]
    unroll_len = actions.shape[1]
    logits = head_out[:, :, :act_count]
    qvalues = head_out[:, :, act_count:]
    exp_logits = jnp.exp(logits)
    policy = exp_logits / jnp.sum(exp_logits, axis=-1, keepdims=True)
    values = jnp.sum(policy * qvalues, axis=-1)
    onehot_f = (
        jnp.transpose(actions)[:, :, None] == jnp.arange(act_count, dtype=jnp.int32)[None, None, :]
    ).astype(jnp.float32)
    logpol = logits[:unroll_len] - jnp.log(jnp.sum(exp_logits[:unroll_len], axis=-1, keepdims=True))
    behave = jnp.transpose(behaviour, (1, 0, 2))
    behave_log = behave - jnp.log(jnp.sum(jnp.exp(behave), axis=-1, keepdims=True))
    ratios = jnp.exp(jnp.sum(onehot_f * (logpol - behave_log), axis=-1))
    clipped = jnp.minimum(1.0, ratios)
    not_ended = 1.0 - jnp.transpose(ends).astype(jnp.float32)
    td_error = jnp.transpose(rewards) + DISCOUNT * not_ended * values[1:] - values[:unroll_len]
    carried = jnp.zeros_like(values[0])
    collected = []
    for step in range(unroll_len - 1, -1, -1):
        carried = (
            clipped[step] * td_error[step]
            + DISCOUNT * TRACE_LAMBDA * not_ended[step] * clipped[step] * carried
        )
        collected.append(carried)
    collected = jnp.stack(collected[::-1])
    targets = values[:unroll_len] + collected
    advantage = qvalues[:unroll_len] - values[:unroll_len, :, None]
    return (policy[:unroll_len], onehot_f, targets, advantage)


def objective(head_out, onehot_f, targets, cmpo_policy, taken_weight, norm_scale):
    act_count = onehot_f.shape[-1]
    unroll_len = onehot_f.shape[0]
    logits = head_out[:unroll_len, :, :act_count]
    qvalues = head_out[:unroll_len, :, act_count:]
    logpol = logits - jnp.log(jnp.sum(jnp.exp(logits), axis=-1, keepdims=True))
    q_taken = jnp.sum(onehot_f * qvalues, axis=-1)
    value_term = 0.5 * (q_taken - targets) ** 2
    policy_term = -taken_weight * jnp.sum(onehot_f * logpol, axis=-1)
    regular = -jnp.sum(cmpo_policy * logpol, axis=-1)
    return jnp.sum(value_term + policy_term + regular) * norm_scale


def backward(cotangent, rounded, squashed, onehot, w_hidden, w_heads):
    unroll_len = len(squashed)
    hid = w_hidden.shape[0]
    grad_state = jnp.zeros(squashed[0].shape, jnp.float32)
    grad_hidden = jnp.zeros((hid, hid), jnp.float32)
    grad_action = jnp.zeros((hid, onehot.shape[-1]), jnp.float32)
    grad_heads = jnp.zeros(w_heads.shape, jnp.float32)
    for step in range(unroll_len - 1, -1, -1):
        grad_pre = (grad_state * (1.0 - squashed[step] * squashed[step])).astype(jnp.bfloat16)
        head_cot = cotangent[step].astype(jnp.bfloat16)
        grad_hidden = grad_hidden + jnp.dot(
            rounded[step].T, grad_pre, preferred_element_type=jnp.float32
        )
        grad_action = grad_action + jnp.dot(
            grad_pre.T, onehot[:, step], preferred_element_type=jnp.float32
        )
        grad_heads = grad_heads + jnp.dot(
            rounded[step].T, head_cot, preferred_element_type=jnp.float32
        )
        grad_state = grad_state + jnp.dot(grad_pre, w_hidden.T, preferred_element_type=jnp.float32)
        grad_state = grad_state + jnp.dot(head_cot, w_heads.T, preferred_element_type=jnp.float32)
    return (grad_hidden, grad_action, grad_heads)


def body(embed, actions, rewards, ends, behaviour, w_hidden, w_action, w_heads):
    rows_here = embed.shape[0]
    unroll_len = actions.shape[1]
    act_count = w_action.shape[0]
    groups = lax.axis_size("batch")
    devices = lax.axis_size("rep") * groups
    head_out, rounded, squashed, onehot = unroll(embed, actions, w_hidden, w_action, w_heads)
    policy, onehot_f, targets, advantage = estimates(head_out, actions, rewards, ends, behaviour)
    spread = lax.psum(jnp.sum(advantage * advantage), "batch")
    spread_scale = jnp.sqrt(spread / (groups * rows_here * unroll_len * act_count) + EPSILON)
    weights = jnp.exp(jnp.clip(advantage / spread_scale, -1.0, 1.0))
    norm_mass = jnp.sum(policy * weights, axis=-1)
    mass_sum = lax.psum(jnp.sum(norm_mass), "batch")
    mean_mass = mass_sum / (groups * rows_here * unroll_len)
    cmpo_policy = policy * weights / norm_mass[:, :, None]
    taken_weight = jnp.sum(onehot_f * weights, axis=-1) / mean_mass
    cotangent = jax.grad(objective)(
        head_out,
        onehot_f,
        targets,
        cmpo_policy,
        taken_weight,
        1.0 / (devices * rows_here * unroll_len),
    )
    grad_hidden, grad_action, grad_heads = backward(
        cotangent, rounded, squashed, onehot, w_hidden, w_heads
    )
    grad_hidden, grad_action, grad_heads = lax.psum(
        (grad_hidden, grad_action, grad_heads), ("rep", "batch")
    )
    return (grad_hidden, grad_action.T, grad_heads, targets.T)


def solution(mesh):
    placed = (
        P(("rep", "batch"), None),
        P(("rep", "batch"), None),
        P(("rep", "batch"), None),
        P(("rep", "batch"), None),
        P(("rep", "batch"), None, None),
        P(),
        P(),
        P(),
    )
    return jax.shard_map(
        body,
        mesh=mesh,
        in_specs=placed,
        out_specs=(P(), P(), P(), P(("rep", "batch"), None)),
        check_vma=False,
    )
```

profile of v0, /device:TPU:0, one launch (start us, length us, event | category | flops | bytes accessed | tf_op | source)
XLA Modules:
  0.0 216.6 jit_solution(16951233208367975323)
XLA Ops:
  7.2 0.0 copy-start
  7.2 0.0 all-reduce.5.cloned.1.call-start
  7.2 0.9 iota_compare_fusion.1
  8.1 0.7 copy-done
  8.8 1.4 fusion.52
  10.2 0.3 fusion.23
  10.5 0.4 fusion.53
  11.0 0.3 fusion.27
  11.3 0.4 fusion.54
  11.7 1.1 fusion.48
  12.8 0.4 fusion.55
  13.2 0.3 add_convert_fusion.2
  13.6 0.4 fusion.56
  14.0 0.3 fusion.4
  14.3 0.8 fusion.41
  15.1 1.6 fusion.45
  16.7 2.7 %fusion.46 = f32[1024,1024]{1,0:T(8,128)} fusion(bf16[128,1024]{1,0:T(8,128)(2,1)S(1)} %get-tuple-element.46, f32[128,1024]{1,0:T(8,128)S(1)} %fusion.4), kind=kOutput, calls=%fused_computation.125 | convolution fusion | flops 268959744 | bytes 4980736 | tf_op jit(solution)/shard_map/dot_general | solution.py:90
  19.5 0.2 fusion.20
  19.7 0.2 constant_dynamic-update-slice_fusion.9
  19.9 0.0 copy-done.4
  19.9 0.2 constant_dynamic-update-slice_fusion.8
  20.1 0.2 constant_dynamic-update-slice_fusion.7
  20.3 0.2 constant_dynamic-update-slice_fusion.6
  20.5 0.0 copy-done.6
  20.5 0.2 constant_dynamic-update-slice_fusion.5
  20.7 0.0 copy-start.14
  20.7 0.2 fusion.21
  21.0 0.7 slice_exponential_fusion
  21.6 0.6 multiply_reduce_fusion
  22.3 9.0 %psum.35 = f32[]{:T(128)} all-reduce(f32[]{:T(128)} %multiply_reduce_fusion), channel_id=1, replica_groups=mesh['rep'=8,'batch'=4] {'batch'}, use_global_device_ids=true, to_apply=%region_7.8 | all-reduce | flops 1 | bytes 8 | tf_op jit(solution)/shard_map/psum | solution.py:112
  32.1 2.2 %select_reduce_fusion.1 = (f32[5,128]{1,0:T(8,128)S(1)}, f32[5,128]{1,0:T(8,128)}, f32[5,128]{1,0:T(8,128)}, f32[]{:T(128)}, f32[5,128,18]{1,2,0:T(8,128)}) fusion(f32[5,128,36]{1,2,0:T(8,128)} %copy-done.14, s32[5,128]{1,0:T(8,128)S(1)} %bitcast.143, f32[]{:T(128)S(6)} %sqrt.3, f32[5,128]{1,0:T(8,128)S(1)} %get-tuple-element.40, ...), kind=kLoop, calls=%fused_computation.71 | loop fusion | flops 124799 | bytes 197128 | tf_op jit(solution)/shard_map/jvp()/reduce_sum | solution.py:73
  34.2 6.4 %psum.36 = f32[]{:T(128)} all-reduce(f32[]{:T(128)} %get-tuple-element.25), channel_id=1, replica_groups=mesh['rep'=8,'batch'=4] {'batch'}, use_global_device_ids=true, to_apply=%region_11.12 | all-reduce | flops 1 | bytes 8 | tf_op jit(solution)/shard_map/psum | solution.py:116
  40.7 0.6 add_bitcast_fusion
  42.1 0.8 negate_multiply_fusion
  42.8 0.9 fusion.50
  43.8 0.7 negate_divide_fusion
  44.5 0.9 multiply_add_fusion
  45.3 1.1 fusion.60
  46.5 0.2 convolution_add_fusion.14
  46.6 0.2 convolution_add_fusion.13
  46.8 0.2 convolution_add_fusion.12
  47.0 0.8 fusion.10
  47.9 0.3 multiply_convert_fusion.2
  48.1 0.7 fusion.57
  48.9 0.8 convolution_add_fusion.6
  49.7 0.2 copy-done.11
  49.9 0.3 multiply_convert_fusion.1
  50.2 0.7 fusion.58
  50.9 0.8 convolution_add_fusion.5
  51.7 0.2 copy-done.8
  51.9 0.3 multiply_convert_fusion
  52.2 0.7 fusion.59
  53.0 0.8 convolution_add_fusion.4
  53.8 0.3 fusion.9
  54.1 0.2 convolution_add_fusion.18
  54.2 0.2 convolution_add_fusion.17
  54.4 0.2 convolution_add_fusion.16
  54.6 0.8 fusion.11
  55.4 3.1 %bitcast_add_fusion = f32[1024,1024]{1,0:T(8,128)} fusion(f32[1024,1024]{1,0:T(8,128)S(1)} %fusion.59, f32[1024,1024]{1,0:T(8,128)S(1)} %fusion.58, f32[1024,1024]{1,0:T(8,128)S(1)} %copy-done.1, f32[1024,1024]{1,0:T(8,128)S(1)} %fusion.57, bf16[128,1024]{1,0:T(8,128)(2,1)S(1)} %fusion.9, bf16[128,1024]{1,0:T(8,128)(2,1)S(1)} %copy-done.2), kind=kOutput, calls=%fused_computation.3 | convolution fusion | flops 272629760 | bytes 21495808 | tf_op jit(solution)/shard_map/dot_general | solution.py:90
  58.4 0.0 all-reduce.5.cloned.1.call-update
  58.4 145.2 %all-reduce.5.cloned.1.call-done = (f32[1024,1024]{1,0:T(8,128)}, f32[18,1024]{1,0:T(8,128)}, f32[1024,36]{0,1:T(8,128)}) async-done(((f32[1024,1024]{1,0:T(8,128)}, f32[18,1024]{1,0:T(8,128)}, f32[1024,36]{0,1:T(8,128)}), (f32[1024,1024]{1,0:T(8,128)}, f32[18,1024]{1,0:T(8,128)}, f32[1024,36]{0,1:T(8,128)})) %all-reduce.5.cloned.1.call-update) | async-done | bytes 4415504 | tf_op jit(solution)/shard_map/psum | solution.py:131
  203.6 4.8 %copy.28 = f32[1024,1024]{1,0:T(8,128)} copy(f32[1024,1024]{1,0:T(8,128)} %get-tuple-element.57) | data formatting | bytes 8388608
  208.4 0.6 copy.29
  209.1 0.7 copy.30
  (49 shorter events, 0.2 us)
Async XLA Ops:
  7.2 1.6 copy-start
  7.2 3.0 %copy-start.2 = (bf16[128,1024]{1,0:T(8,128)(2,1)S(1)}, bf16[128,1024]{1,0:T(8,128)(2,1)}, u32[]{:S(2)}) copy-start(bf16[128,1024]{1,0:T(8,128)(2,1)} %param.8) | copy-start | bytes 786436
  7.2 3.0 %copy-start.13 = (bf16[18,1024]{1,0:T(8,128)(2,1)S(1)}, bf16[18,1024]{1,0:T(8,128)(2,1)}, u32[]{:S(2)}) copy-start(bf16[18,1024]{1,0:T(8,128)(2,1)} %param.14) | copy-start | bytes 110596
  7.2 196.4 %all-reduce.5.cloned.1.call-start = ((), (), s32[]{:S(2)}) async-start(), calls=%async_computation | async-start | bytes 8912896 | tf_op jit(solution)/shard_map/psum | solution.py:131
  8.8 5.5 %copy-start.17 = (pred[128,5,18]{0,2,1:T(8,128)(4,1)}, pred[128,5,18]{0,2,1:T(8,128)(4,1)S(1)}, u32[]{:S(2)}) copy-start(pred[128,5,18]{0,2,1:T(8,128)(4,1)S(1)} %iota_compare_fusion.1) | copy-start | bytes 34564
  10.5 9.4 %copy-start.4 = (bf16[128,1024]{1,0:T(8,128)(2,1)}, bf16[128,1024]{1,0:T(8,128)(2,1)S(1)}, u32[]{:S(2)}) copy-start(bf16[128,1024]{1,0:T(8,128)(2,1)S(1)} %get-tuple-element.41) | copy-start | bytes 786436
  11.2 1.5 copy-start.7
  13.5 7.0 %copy-start.6 = (bf16[128,1024]{1,0:T(8,128)(2,1)}, bf16[128,1024]{1,0:T(8,128)(2,1)S(1)}, u32[]{:S(2)}) copy-start(bf16[128,1024]{1,0:T(8,128)(2,1)S(1)} %get-tuple-element.46) | copy-start | bytes 786436
  13.5 7.2 %copy-start.9 = (f32[128,1024]{1,0:T(8,128)}, f32[128,1024]{1,0:T(8,128)S(1)}, u32[]{:S(2)}) copy-start(f32[128,1024]{1,0:T(8,128)S(1)} %get-tuple-element.47) | copy-start | bytes 1572868
  16.7 2.8 %copy-start.22 = (s32[128,5]{0,1:T(8,128)S(1)}, s32[128,5]{0,1:T(8,128)}, u32[]{:S(2)}) copy-start(s32[128,5]{0,1:T(8,128)} %param.11) | copy-start | bytes 7684
  16.7 2.8 %copy-start.21 = (f32[128,5,18]{0,2,1:T(8,128)S(1)}, f32[128,5,18]{0,2,1:T(8,128)}, u32[]{:S(2)}) copy-start(f32[128,5,18]{0,2,1:T(8,128)} %param.12) | copy-start | bytes 138244
  16.7 2.9 %copy-start.3 = (bf16[1024,36]{0,1:T(8,128)(2,1)S(1)}, bf16[1024,36]{0,1:T(8,128)(2,1)}, u32[]{:S(2)}) copy-start(bf16[1024,36]{0,1:T(8,128)(2,1)} %param.15) | copy-start | bytes 221188
  19.5 2.1 copy-start.23
  19.5 2.8 %copy-start.20 = (s32[128,5]{0,1:T(8,128)S(1)}, s32[128,5]{0,1:T(8,128)}, u32[]{:S(2)}) copy-start(s32[128,5]{0,1:T(8,128)} %param.9) | copy-start | bytes 7684
  20.7 1.6 copy-start.14
  42.0 4.8 %copy-start.5 = (bf16[128,1024]{1,0:T(8,128)(2,1)S(1)}, bf16[128,1024]{1,0:T(8,128)(2,1)}, u32[]{:S(2)}) copy-start(bf16[128,1024]{1,0:T(8,128)(2,1)} %copy-done.4) | copy-start | bytes 786436
  42.0 5.8 %copy-start.10 = (f32[128,1024]{1,0:T(8,128)S(1)}, f32[128,1024]{1,0:T(8,128)}, u32[]{:S(2)}) copy-start(f32[128,1024]{1,0:T(8,128)} %copy-done.9) | copy-start | bytes 1572868
  42.0 5.8 %copy-start.12 = (f32[128,1024]{1,0:T(8,128)S(1)}, f32[128,1024]{1,0:T(8,128)}, u32[]{:S(2)}) copy-start(f32[128,1024]{1,0:T(8,128)} %fusion.45) | copy-start | bytes 1572868
  48.8 1.0 copy-start.11
  50.9 1.0 copy-start.8
  52.9 1.1 copy-start.15
  52.9 1.1 copy-start.18
  52.9 2.4 %copy-start.1 = (f32[1024,1024]{1,0:T(8,128)S(1)}, f32[1024,1024]{1,0:T(8,128)}, u32[]{:S(2)}) copy-start(f32[1024,1024]{1,0:T(8,128)} %fusion.46) | copy-start | bytes 12582916
  203.6 4.8 %copy-start.19 = (f32[18,1024]{1,0:T(8,128)S(1)}, f32[18,1024]{1,0:T(8,128)}, u32[]{:S(2)}) copy-start(f32[18,1024]{1,0:T(8,128)} %get-tuple-element.58) | copy-start | bytes 221188
  203.6 5.5 %copy-start.16 = (f32[1024,36]{0,1:T(8,128)S(1)}, f32[1024,36]{0,1:T(8,128)}, u32[]{:S(2)}) copy-start(f32[1024,36]{0,1:T(8,128)} %get-tuple-element.59) | copy-start | bytes 442372
Sparse Core Ops, SparseCore 0:
  58.6 145.0 all-reduce.4
where the time goes:
time: 217 us
  waiting for transfers between devices  145 us (67%)
  matrix products  24.2 us (11%)
  between operations  15.9 us (7%)
  blocking collectives  15.5 us (7%)
  other arithmetic  8.42 us (4%)
  local copies, waits for them, and re-layouts  7.38 us (3%)
    psum x1, waiting for transfers between devices, body(): lax.psum((grad_hidden, grad_action, grad_heads), ('rep', 'batch'))  145 us
    psum x1, blocking collectives, body(): spread = lax.psum(jnp.sum(advantage * advantage), 'batch')  9.04 us
    dot_general x5, matrix products, backward(): jnp.dot(rounded[step].T, grad_pre, preferred_element_type=jnp.float32)  7.97 us
    unnamed x51, local copies, waits for them, and re-layouts  7.36 us
    psum x1, blocking collectives, body(): mass_sum = lax.psum(jnp.sum(norm_mass), 'batch')  6.44 us
  transfers between devices with their start and end apart: 1, of which 1 were waited for; matrix products, arithmetic and copies ran while one was open for 0% of the time, Pallas kernels for 0%

commit v1 on v0

--- a/solution.py
+++ b/solution.py
@@ -1,3 +1,4 @@
+import functools
 import jax
 import jax.numpy as jnp
 from jax import lax
@@ -6,6 +7,15 @@
 DISCOUNT = 0.997
 TRACE_LAMBDA = 0.95
 EPSILON = 1e-06
+
+
+def _take_inputs(here_x, group_axis, mesh_dim):
+    reached = lax.psum(here_x, group_axis)
+    inter = lax.psum(reached, mesh_dim)
+    return inter
+
+
+resolve_the_ways = functools.partial(_take_inputs, group_axis="batch", mesh_dim="rep")
 
 
 def unroll(emb_block, act_block, w_hidden, w_action, w_heads):
@@ -128,9 +138,7 @@
     grad_hidden, grad_action, grad_heads = backward(
         cotangent, rounded, squashed, onehot, w_hidden, w_heads
     )
-    grad_hidden, grad_action, grad_heads = lax.psum(
-        (grad_hidden, grad_action, grad_heads), ("rep", "batch")
-    )
+    grad_hidden, grad_action, grad_heads = resolve_the_ways((grad_hidden, grad_action, grad_heads))
     return (grad_hidden, grad_action.T, grad_heads, targets.T)
 
 

time: 217 us -> 329 us (1.52)
  waiting for transfers between devices: 145 us -> 257 us
    psum x1 -> x2, waiting for transfers between devices: 145 us -> 257 us  [the longest x1 167 us: _take_inputs(): inter = lax.psum(reached, mesh_dim)]
  transfers between devices with their start and end apart: 1 -> 2, of which waited for: 1 -> 2; matrix products, arithmetic and copies ran while one was open for 0% -> 0% of each run, Pallas kernels for 0% -> 0%
where the time goes in v1:
time: 329 us
  waiting for transfers between devices  257 us (78%)
  matrix products  24.2 us (7%)
  between operations  15.8 us (5%)
  blocking collectives  15.5 us (5%)
  other arithmetic  8.41 us (3%)
  local copies, waits for them, and re-layouts  7.38 us (2%)
    psum x1, waiting for transfers between devices, _take_inputs(): inter = lax.psum(reached, mesh_dim)  167 us
    psum x1, waiting for transfers between devices, _take_inputs(): reached = lax.psum(here_x, group_axis)  90.3 us
    psum x1, blocking collectives, body(): spread = lax.psum(jnp.sum(advantage * advantage), 'batch')  9.04 us
    dot_general x5, matrix products, backward(): jnp.dot(rounded[step].T, grad_pre, preferred_element_type=jnp.float32)  7.97 us
    unnamed x51, local copies, waits for them, and re-layouts  7.36 us
  transfers between devices with their start and end apart: 2, of which 2 were waited for; matrix products, arithmetic and copies ran while one was open for 0% of the time, Pallas kernels for 0%

profile of v1, /device:TPU:0, one launch (start us, length us, event | category | flops | bytes accessed | tf_op | source)
XLA Modules:
  0.0 328.7 jit_solution(7001495794788595772)
XLA Ops:
  7.2 0.0 all-reduce.9.cloned.1.call-start
  7.2 0.9 iota_compare_fusion.1
  8.1 0.7 copy-done
  8.8 1.4 fusion.51
  10.2 0.3 fusion.22
  10.5 0.4 fusion.52
  11.0 0.3 fusion.26
  11.3 0.4 fusion.53
  11.7 1.1 fusion.47
  12.8 0.4 fusion.54
  13.3 0.3 add_convert_fusion.2
  13.6 0.4 fusion.55
  14.0 0.3 fusion.4
  14.3 0.8 fusion.40
  15.1 1.6 fusion.44
  16.8 2.7 fusion.45
  19.5 0.2 fusion.19
  19.7 0.2 constant_dynamic-update-slice_fusion.9
  19.9 0.0 copy-done.4
  19.9 0.2 constant_dynamic-update-slice_fusion.8
  20.1 0.2 constant_dynamic-update-slice_fusion.7
  20.3 0.2 constant_dynamic-update-slice_fusion.6
  20.5 0.0 copy-done.6
  20.5 0.2 constant_dynamic-update-slice_fusion.5
  20.7 0.0 copy-start.14
  20.7 0.2 fusion.20
  21.0 0.7 slice_exponential_fusion
  21.6 0.6 multiply_reduce_fusion
  22.3 9.0 %psum.56 = f32[]{:T(128)} all-reduce(f32[]{:T(128)} %multiply_reduce_fusion), channel_id=1, replica_groups=mesh['rep'=8,'batch'=4] {'batch'}, use_global_device_ids=true, to_apply=%region_7.8 | all-reduce | flops 1 | bytes 8 | tf_op jit(solution)/shard_map/psum | solution.py:122
  32.1 2.2 select_reduce_fusion.1
  34.2 6.4 %psum.57 = f32[]{:T(128)} all-reduce(f32[]{:T(128)} %get-tuple-element.28), channel_id=1, replica_groups=mesh['rep'=8,'batch'=4] {'batch'}, use_global_device_ids=true, to_apply=%region_11.12 | all-reduce | flops 1 | bytes 8 | tf_op jit(solution)/shard_map/psum | solution.py:126
  40.7 0.6 add_bitcast_fusion
  42.0 0.8 negate_multiply_fusion
  42.8 0.9 fusion.49
  43.7 0.7 negate_divide_fusion
  44.4 0.9 multiply_add_fusion
  45.3 1.1 fusion.59
  46.4 0.2 convolution_add_fusion.14
  46.6 0.2 convolution_add_fusion.13
  46.8 0.2 convolution_add_fusion.12
  46.9 0.8 fusion.10
  47.8 0.3 multiply_convert_fusion.2
  48.0 0.7 fusion.56
  48.8 0.8 convolution_add_fusion.6
  49.6 0.2 copy-done.11
  49.8 0.3 multiply_convert_fusion.1
  50.1 0.7 fusion.57
  50.8 0.8 convolution_add_fusion.5
  51.7 0.2 copy-done.8
  51.9 0.3 multiply_convert_fusion
  52.1 0.7 fusion.58
  52.9 0.8 convolution_add_fusion.4
  53.7 0.3 fusion.9
  54.0 0.2 convolution_add_fusion.18
  54.2 0.2 convolution_add_fusion.17
  54.3 0.2 convolution_add_fusion.16
  54.5 0.8 convolution_add_fusion.15
  55.3 3.1 bitcast_add_fusion
  58.4 0.0 all-reduce.7.cloned.1.call-start
  58.4 90.3 %all-reduce.9.cloned.1.call-done = (f32[1024,1024]{1,0:T(8,128)}, f32[1024,18]{0,1:T(8,128)}, f32[1024,36]{0,1:T(8,128)}) async-done(((f32[1024,1024]{1,0:T(8,128)}, f32[1024,18]{0,1:T(8,128)}, f32[1024,36]{0,1:T(8,128)}), (f32[1024,1024]{1,0:T(8,128)}, f32[1024,18]{0,1:T(8,128)}, f32[1024,36]{0,1:T(8,128)})) %all-reduce.9.cloned.1.call-update) | async-done | bytes 4415504 | tf_op jit(solution)/shard_map/psum | solution.py:13
  148.7 167.1 %all-reduce.7.cloned.1.call-done = (f32[1024,1024]{1,0:T(8,128)}, f32[18,1024]{1,0:T(8,128)}, f32[1024,36]{0,1:T(8,128)}) async-done(((f32[1024,1024]{1,0:T(8,128)}, f32[18,1024]{1,0:T(8,128)}, f32[1024,36]{0,1:T(8,128)}), (f32[1024,1024]{1,0:T(8,128)}, f32[18,1024]{1,0:T(8,128)}, f32[1024,36]{0,1:T(8,128)})) %all-reduce.7.cloned.1.call-update) | async-done | bytes 4415504 | tf_op jit(solution)/shard_map/psum | solution.py:14
  315.8 4.8 %copy.31 = f32[1024,1024]{1,0:T(8,128)} copy(f32[1024,1024]{1,0:T(8,128)} %get-tuple-element.60) | data formatting | bytes 8388608
  320.6 0.6 copy.32
  321.2 0.7 copy.33
  (52 shorter events, 0.3 us)
Async XLA Ops:
  7.2 1.6 copy-start
  7.2 3.0 copy-start.2
  7.2 3.0 copy-start.13
  7.2 141.5 %all-reduce.9.cloned.1.call-start = ((), (), s32[]{:S(2)}) async-start(), calls=%async_computation.1 | async-start | bytes 8912896 | tf_op jit(solution)/shard_map/psum | solution.py:13
  8.8 5.5 %copy-start.17 = (pred[128,5,18]{0,2,1:T(8,128)(4,1)}, pred[128,5,18]{0,2,1:T(8,128)(4,1)S(1)}, u32[]{:S(2)}) copy-start(pred[128,5,18]{0,2,1:T(8,128)(4,1)S(1)} %iota_compare_fusion.1) | copy-start | bytes 34564
  10.5 9.4 %copy-start.4 = (bf16[128,1024]{1,0:T(8,128)(2,1)}, bf16[128,1024]{1,0:T(8,128)(2,1)S(1)}, u32[]{:S(2)}) copy-start(bf16[128,1024]{1,0:T(8,128)(2,1)S(1)} %get-tuple-element.44) | copy-start | bytes 786436
  11.2 1.6 copy-start.7
  13.5 7.0 %copy-start.6 = (bf16[128,1024]{1,0:T(8,128)(2,1)}, bf16[128,1024]{1,0:T(8,128)(2,1)S(1)}, u32[]{:S(2)}) copy-start(bf16[128,1024]{1,0:T(8,128)(2,1)S(1)} %get-tuple-element.49) | copy-start | bytes 786436
  13.6 7.2 %copy-start.9 = (f32[128,1024]{1,0:T(8,128)}, f32[128,1024]{1,0:T(8,128)S(1)}, u32[]{:S(2)}) copy-start(f32[128,1024]{1,0:T(8,128)S(1)} %get-tuple-element.50) | copy-start | bytes 1572868
  16.7 2.8 copy-start.22
  16.7 2.8 copy-start.21
  16.7 2.9 copy-start.3
  19.5 2.1 copy-start.23
  19.5 2.8 copy-start.20
  20.7 1.6 copy-start.14
  42.0 4.8 %copy-start.5 = (bf16[128,1024]{1,0:T(8,128)(2,1)S(1)}, bf16[128,1024]{1,0:T(8,128)(2,1)}, u32[]{:S(2)}) copy-start(bf16[128,1024]{1,0:T(8,128)(2,1)} %copy-done.4) | copy-start | bytes 786436
  42.0 5.8 %copy-start.10 = (f32[128,1024]{1,0:T(8,128)S(1)}, f32[128,1024]{1,0:T(8,128)}, u32[]{:S(2)}) copy-start(f32[128,1024]{1,0:T(8,128)} %copy-done.9) | copy-start | bytes 1572868
  42.0 5.8 %copy-start.12 = (f32[128,1024]{1,0:T(8,128)S(1)}, f32[128,1024]{1,0:T(8,128)}, u32[]{:S(2)}) copy-start(f32[128,1024]{1,0:T(8,128)} %fusion.44) | copy-start | bytes 1572868
  48.8 1.0 copy-start.11
  50.8 1.0 copy-start.8
  52.8 1.1 copy-start.15
  52.9 1.1 copy-start.18
  52.9 2.4 copy-start.1
  58.4 257.4 %all-reduce.7.cloned.1.call-start = ((), (), s32[]{:S(2)}) async-start(), calls=%async_computation | async-start | bytes 8912896 | tf_op jit(solution)/shard_map/psum | solution.py:14
  315.8 4.8 %copy-start.19 = (f32[18,1024]{1,0:T(8,128)S(1)}, f32[18,1024]{1,0:T(8,128)}, u32[]{:S(2)}) copy-start(f32[18,1024]{1,0:T(8,128)} %get-tuple-element.61) | copy-start | bytes 221188
  315.8 5.5 %copy-start.16 = (f32[1024,36]{0,1:T(8,128)S(1)}, f32[1024,36]{0,1:T(8,128)}, u32[]{:S(2)}) copy-start(f32[1024,36]{0,1:T(8,128)} %get-tuple-element.62) | copy-start | bytes 442372
Sparse Core Ops, SparseCore 0:
  58.5 90.1 all-reduce.8
  152.6 163.1 all-reduce.6
